TPU v7x, 32 devices: a whole 2x2x4 slice. The times are simulated.
32 devices in a mesh: grp: 2 (over y), col: 4 (over z), seq: 4 (over x, core).
Axes of the slice: x: 2, y: 2, z: 4, core: 2. Of those that a mesh axis runs over, the one named last changes fastest.
Arguments:
- row_query: bfloat16 [256, 16, 768], P(('grp', 'seq'), 'col'), parts along dimension 0, may hold values from -6 to 6
- row_key: bfloat16 [256, 16, 768], P(('grp', 'seq'), 'col'), parts along dimension 0, may hold values from -6 to 6
- row_value: bfloat16 [256, 16, 768], P(('grp', 'seq'), 'col'), parts along dimension 0, may hold values from -6 to 6
- row_grad: bfloat16 [256, 16, 768], P(('grp', 'seq'), 'col'), parts along dimension 0, may hold values from -48 to 48
- col_query: bfloat16 [256, 16, 768], P(('grp', 'seq'), 'col'), parts along dimension 0, may hold values from -11 to 11
- col_key: bfloat16 [256, 16, 768], P(('grp', 'seq'), 'col'), parts along dimension 0, may hold values from -11 to 11
- col_value: bfloat16 [256, 16, 768], P(('grp', 'seq'), 'col'), parts along dimension 0, may hold values from -6 to 6
- col_grad: bfloat16 [256, 16, 768], P(('grp', 'seq'), 'col'), parts along dimension 0, may hold values from -48 to 48
Outputs:
- row_dquery: bfloat16 [256, 16, 768], P(('grp', 'seq'), 'col'), parts along dimension 0
- row_dkey: bfloat16 [256, 16, 768], P(('grp', 'seq'), 'col'), parts along dimension 0
- row_dvalue: bfloat16 [256, 16, 768], P(('grp', 'seq'), 'col'), parts along dimension 0
- col_dquery: bfloat16 [256, 16, 768], P(('grp', 'seq'), 'col'), parts along dimension 0
- col_dkey: bfloat16 [256, 16, 768], P(('grp', 'seq'), 'col'), parts along dimension 0
- col_dvalue: bfloat16 [256, 16, 768], P(('grp', 'seq'), 'col'), parts along dimension 0
There are 2 independent parts, one for each index of `grp`. A program takes and returns all parts, laid end to end along the dimension named above; each array names one. Nothing has to cross between parts.
All inputs are finite; a program needn't handle non-finite values.
Results may differ from a plain program's by a relative error of at most 0.009.
Values may be sent and summed in bfloat16 or wider, within the bound.
No kernel may reach another device: no remote copies, remote signals or barrier semaphores. Data moves between devices by JAX's collectives and lax.ppermute only.
A program may use at most 64 MiB of HBM per device.

v0:
```python
import jax
import jax.numpy as jnp
from jax import lax
from jax.sharding import PartitionSpec as P

HEADS = 12
HEAD = 64


def tied_terms(scores, prob_grad, row_scale):
    row_probs = jax.nn.softmax(scores, axis=-1)
    row_delta = jnp.sum(row_probs * prob_grad, axis=-1, keepdims=True)
    score_gradient_part = row_probs * (prob_grad - row_delta) * row_scale
    return (row_probs.astype(jnp.bfloat16), score_gradient_part.astype(jnp.bfloat16))


def split_heads(block):
    return block.reshape(block.shape[0], block.shape[1] // HEAD, HEAD)


def column_core(query_row_block, key_row_block, value_row_block, gradient_row_block, col_scale):
    scores = (
        jnp.einsum(
            "qzd,izd->zqi", query_row_block, key_row_block, preferred_element_type=jnp.float32
        )
        * col_scale
    )
    prob_grad = jnp.einsum(
        "qzd,izd->zqi", gradient_row_block, value_row_block, preferred_element_type=jnp.float32
    )
    col_probs = jax.nn.softmax(scores, axis=-1)
    col_delta = jnp.sum(col_probs * prob_grad, axis=-1, keepdims=True)
    score_gradient_part = (col_probs * (prob_grad - col_delta) * col_scale).astype(jnp.bfloat16)
    attention_weight_rows = col_probs.astype(jnp.bfloat16)
    query_grad = jnp.einsum(
        "qvc,cqb->vqb", score_gradient_part, key_row_block, preferred_element_type=jnp.float32
    )
    key_gradient_part = jnp.einsum(
        "wzc,zwi->cwi", score_gradient_part, query_row_block, preferred_element_type=jnp.float32
    )
    value_gradient_part = jnp.einsum(
        "wzc,zwi->cwi",
        attention_weight_rows,
        gradient_row_block,
        preferred_element_type=jnp.float32,
    )
    return (
        query_grad.astype(jnp.bfloat16),
        key_gradient_part.astype(jnp.bfloat16),
        value_gradient_part.astype(jnp.bfloat16),
    )


def local(row_query, row_key, row_value, row_grad, col_query, col_key, col_value, col_grad):
    seq_dev, col_dev, width = row_query.shape
    seqs = seq_dev * lax.axis_size("seq")
    cols = col_dev * lax.axis_size("col")
    row_scale = HEAD ** (-0.5) * seqs ** (-0.5)
    col_scale = HEAD ** (-0.5)
    moved = (
        lax.all_to_all(row_query, "col", split_axis=0, concat_axis=1, tiled=True),
        lax.all_to_all(row_key, "col", split_axis=0, concat_axis=1, tiled=True),
        lax.all_to_all(row_value, "col", split_axis=0, concat_axis=1, tiled=True),
        lax.all_to_all(row_grad, "col", split_axis=0, concat_axis=1, tiled=True),
    )
    own_rows = moved[0].shape[0]
    shape_four = (own_rows, cols, HEADS, HEAD)
    query_row_block = moved[0].reshape(shape_four)
    key_row_block = moved[1].reshape(shape_four)
    value_row_block = moved[2].reshape(shape_four)
    gradient_row_block = moved[3].reshape(shape_four)
    score_part = (
        jnp.einsum(
            "sihe,sjhe->hij", query_row_block, key_row_block, preferred_element_type=jnp.float32
        )
        * row_scale
    )
    prob_part = jnp.einsum(
        "sihe,sjhe->hij", gradient_row_block, value_row_block, preferred_element_type=jnp.float32
    )
    scores, prob_grad = lax.psum((score_part, prob_part), ("col", "seq"))
    attention_weight_rows, score_gradient_part = tied_terms(scores, prob_grad, row_scale)
    query_grad = jnp.einsum(
        "hij,sjhe->sihe", score_gradient_part, key_row_block, preferred_element_type=jnp.float32
    )
    key_gradient_part = jnp.einsum(
        "hij,sihe->sjhe", score_gradient_part, query_row_block, preferred_element_type=jnp.float32
    )
    value_gradient_part = jnp.einsum(
        "hij,sihe->sjhe",
        attention_weight_rows,
        gradient_row_block,
        preferred_element_type=jnp.float32,
    )
    row_back = (
        lax.all_to_all(
            query_grad.astype(jnp.bfloat16).reshape(own_rows, cols, width),
            "col",
            split_axis=1,
            concat_axis=0,
            tiled=True,
        ),
        lax.all_to_all(
            key_gradient_part.astype(jnp.bfloat16).reshape(own_rows, cols, width),
            "col",
            split_axis=1,
            concat_axis=0,
            tiled=True,
        ),
        lax.all_to_all(
            value_gradient_part.astype(jnp.bfloat16).reshape(own_rows, cols, width),
            "col",
            split_axis=1,
            concat_axis=0,
            tiled=True,
        ),
    )
    flat_width = col_dev * width
    col_moved = (
        lax.all_to_all(
            col_query.reshape(seq_dev, flat_width), "seq", split_axis=1, concat_axis=0, tiled=True
        ),
        lax.all_to_all(
            col_key.reshape(seq_dev, flat_width), "seq", split_axis=1, concat_axis=0, tiled=True
        ),
        lax.all_to_all(
            col_value.reshape(seq_dev, flat_width), "seq", split_axis=1, concat_axis=0, tiled=True
        ),
        lax.all_to_all(
            col_grad.reshape(seq_dev, flat_width), "seq", split_axis=1, concat_axis=0, tiled=True
        ),
    )
    col_grads = column_core(
        split_heads(col_moved[0]),
        split_heads(col_moved[1]),
        split_heads(col_moved[2]),
        split_heads(col_moved[3]),
        col_scale,
    )
    share_width = col_moved[0].shape[1]
    col_back = (
        lax.all_to_all(
            col_grads[0].reshape(seqs, share_width), "seq", split_axis=0, concat_axis=1, tiled=True
        ),
        lax.all_to_all(
            col_grads[1].reshape(seqs, share_width), "seq", split_axis=0, concat_axis=1, tiled=True
        ),
        lax.all_to_all(
            col_grads[2].reshape(seqs, share_width), "seq", split_axis=0, concat_axis=1, tiled=True
        ),
    )
    return (
        row_back[0],
        row_back[1],
        row_back[2],
        col_back[0].reshape(seq_dev, col_dev, width),
        col_back[1].reshape(seq_dev, col_dev, width),
        col_back[2].reshape(seq_dev, col_dev, width),
    )


def solution(mesh):
    in_specs = (
        P(("grp", "seq"), "col", None),
        P(("grp", "seq"), "col", None),
        P(("grp", "seq"), "col", None),
        P(("grp", "seq"), "col", None),
        P(("grp", "seq"), "col", None),
        P(("grp", "seq"), "col", None),
        P(("grp", "seq"), "col", None),
        P(("grp", "seq"), "col", None),
    )
    out_specs = (
        P(("grp", "seq"), "col", None),
        P(("grp", "seq"), "col", None),
        P(("grp", "seq"), "col", None),
        P(("grp", "seq"), "col", None),
        P(("grp", "seq"), "col", None),
        P(("grp", "seq"), "col", None),
    )
    return jax.shard_map(local, mesh=mesh, in_specs=in_specs, out_specs=out_specs, check_vma=False)
```

profile of v0, /device:TPU:0, one launch (start us, length us, event | category | flops | bytes accessed | tf_op | source)
XLA Modules:
  0.0 195.9 jit_solution(17410516336404553708)
XLA Ops:
  0.6 1.6 copy.133
  2.3 4.3 %all-to-all-start.8 = ((bf16[32,4,768]{2,0,1:T(8,128)(2,1)}), bf16[32,4,768]{2,0,1:T(8,128)(2,1)S(1)}, u32[]{:S(2)}, u32[]{:S(2)}) async-start(bf16[32,4,768]{2,0,1:T(8,128)(2,1)} %copy.133), calls=%async_computation.8 | async-start | bytes 393216 | tf_op jit(solution)/shard_map/all_to_all | solution.py:123
  6.6 0.7 copy.136
  7.3 4.6 %all-to-all-done.8 = bf16[32,4,768]{2,0,1:T(8,128)(2,1)S(1)} async-done(((bf16[32,4,768]{2,0,1:T(8,128)(2,1)}), bf16[32,4,768]{2,0,1:T(8,128)(2,1)S(1)}, u32[]{:S(2)}, u32[]{:S(2)}) %all-to-all-start.8) | async-done | bytes 196640 | tf_op jit(solution)/shard_map/all_to_all | solution.py:123
  11.9 3.4 %all-to-all-start.9 = ((bf16[32,4,768]{2,0,1:T(8,128)(2,1)}), bf16[32,4,768]{2,0,1:T(8,128)(2,1)S(1)}, u32[]{:S(2)}, u32[]{:S(2)}) async-start(bf16[32,4,768]{2,0,1:T(8,128)(2,1)} %copy.136), calls=%async_computation.9 | async-start | bytes 393216 | tf_op jit(solution)/shard_map/all_to_all | solution.py:129
  15.3 0.7 copy.137
  16.0 4.6 %all-to-all-done.9 = bf16[32,4,768]{2,0,1:T(8,128)(2,1)S(1)} async-done(((bf16[32,4,768]{2,0,1:T(8,128)(2,1)}), bf16[32,4,768]{2,0,1:T(8,128)(2,1)S(1)}, u32[]{:S(2)}, u32[]{:S(2)}) %all-to-all-start.9) | async-done | bytes 196640 | tf_op jit(solution)/shard_map/all_to_all | solution.py:129
  20.6 3.4 %all-to-all-start.10 = ((bf16[32,4,768]{2,0,1:T(8,128)(2,1)}), bf16[32,4,768]{2,0,1:T(8,128)(2,1)S(1)}, u32[]{:S(2)}, u32[]{:S(2)}) async-start(bf16[32,4,768]{2,0,1:T(8,128)(2,1)} %copy.137), calls=%async_computation.10 | async-start | bytes 393216 | tf_op jit(solution)/shard_map/all_to_all | solution.py:126
  24.0 5.2 %all-to-all-done.10 = bf16[32,4,768]{2,0,1:T(8,128)(2,1)S(1)} async-done(((bf16[32,4,768]{2,0,1:T(8,128)(2,1)}), bf16[32,4,768]{2,0,1:T(8,128)(2,1)S(1)}, u32[]{:S(2)}, u32[]{:S(2)}) %all-to-all-start.10) | async-done | bytes 196640 | tf_op jit(solution)/shard_map/all_to_all | solution.py:126
  29.3 7.7 %all_to_all.214 = bf16[32,4,768]{2,0,1:T(8,128)(2,1)S(1)} all-to-all(bf16[32,4,768]{2,0,1:T(8,128)(2,1)S(1)} %copy.132), channel_id=1, replica_groups=mesh['grp'=2,'col'=4,'seq'=4] {'seq'}, dimensions={1} | all-to-all | bytes 393216 | tf_op jit(solution)/shard_map/all_to_all | solution.py:120
  37.0 12.7 %all_to_all.215 = bf16[32,4,768]{2,1,0:T(4,128)(2,1)S(1)} all-to-all(bf16[32,4,768]{2,1,0:T(4,128)(2,1)S(1)} %copy-done.3), channel_id=1, replica_groups=mesh['grp'=2,'col'=4,'seq'=4] {'col'}, dimensions={0} | all-to-all | bytes 393216 | tf_op jit(solution)/shard_map/all_to_all | solution.py:63
  49.7 3.4 %all-to-all-start.2 = ((bf16[32,4,768]{2,1,0:T(4,128)(2,1)}), bf16[32,4,768]{2,1,0:T(4,128)(2,1)S(1)}, u32[]{:S(2)}, u32[]{:S(2)}) async-start(bf16[32,4,768]{2,1,0:T(4,128)(2,1)} %param.11), calls=%async_computation.2 | async-start | bytes 393216 | tf_op jit(solution)/shard_map/all_to_all | solution.py:64
  53.1 0.3 reshape.108
  53.4 0.4 copy.135
  53.8 0.3 reshape.109
  54.1 0.4 copy.138
  54.5 0.3 reshape.110
  54.8 0.3 reshape.107
  55.2 0.4 copy.134
  55.8 3.5 %all-to-all-done.2 = bf16[32,4,768]{2,1,0:T(4,128)(2,1)S(1)} async-done(((bf16[32,4,768]{2,1,0:T(4,128)(2,1)}), bf16[32,4,768]{2,1,0:T(4,128)(2,1)S(1)}, u32[]{:S(2)}, u32[]{:S(2)}) %all-to-all-start.2) | async-done | bytes 196640 | tf_op jit(solution)/shard_map/all_to_all | solution.py:64
  59.4 3.4 %all-to-all-start.1 = ((bf16[32,4,768]{2,1,0:T(4,128)(2,1)}), bf16[32,4,768]{2,1,0:T(4,128)(2,1)S(1)}, u32[]{:S(2)}, u32[]{:S(2)}) async-start(bf16[32,4,768]{2,1,0:T(4,128)(2,1)} %param.9), calls=%async_computation.1 | async-start | bytes 393216 | tf_op jit(solution)/shard_map/all_to_all | solution.py:62
  62.7 0.4 fusion.59
  63.2 0.3 fusion.15
  63.5 5.4 %all-to-all-done.1 = bf16[32,4,768]{2,1,0:T(4,128)(2,1)S(1)} async-done(((bf16[32,4,768]{2,1,0:T(4,128)(2,1)}), bf16[32,4,768]{2,1,0:T(4,128)(2,1)S(1)}, u32[]{:S(2)}, u32[]{:S(2)}) %all-to-all-start.1) | async-done | bytes 196640 | tf_op jit(solution)/shard_map/all_to_all | solution.py:62
  68.9 3.4 %all-to-all-start = ((bf16[32,4,768]{2,1,0:T(4,128)(2,1)}), bf16[32,4,768]{2,1,0:T(4,128)(2,1)S(1)}, u32[]{:S(2)}, u32[]{:S(2)}) async-start(bf16[32,4,768]{2,1,0:T(4,128)(2,1)} %param.8), calls=%async_computation | async-start | bytes 393216 | tf_op jit(solution)/shard_map/all_to_all | solution.py:61
  72.3 0.4 fusion.13
  72.7 0.4 copy.142
  73.1 1.0 all_to_all.191
  74.1 0.4 copy.145
  74.6 1.0 all_to_all.194
  75.5 0.6 fusion.14
  76.2 0.4 copy.148
  76.6 1.0 all_to_all.197
  77.6 0.3 reshape.103
  78.0 0.3 reshape.102
  78.4 0.3 reshape.101
  78.7 3.4 %all-to-all-start.11 = ((bf16[4,32,768]{2,1,0:T(8,128)(2,1)}), bf16[4,32,768]{2,1,0:T(8,128)(2,1)S(1)}, u32[]{:S(2)}, u32[]{:S(2)}) async-start(bf16[4,32,768]{2,1,0:T(8,128)(2,1)} %all_to_all.191), calls=%async_computation.11 | async-start | bytes 393216 | tf_op jit(solution)/shard_map/all_to_all | solution.py:142
  82.1 0.3 reshape.100
  82.5 0.5 fusion.21
  83.0 0.5 convolution_bitcast_fusion
  83.5 64.1 %all-reduce = (f32[12,16,16]{2,1,0:T(8,128)S(1)}, f32[12,16,16]{2,1,0:T(8,128)S(1)}) all-reduce(f32[12,16,16]{2,1,0:T(8,128)S(1)} %convolution_bitcast_fusion, f32[12,16,16]{2,1,0:T(8,128)S(1)} %fusion.21), channel_id=1, replica_groups=mesh['grp'=2,'col'=4,'seq'=4] {'col','seq'}, use_global_device_ids=true, to_apply=%region_3.0 | all-reduce | flops 6144 | bytes 49152 | tf_op jit(solution)/shard_map/psum | solution.py:81
  147.6 3.4 %all-to-all-start.12 = ((bf16[4,32,768]{2,1,0:T(8,128)(2,1)}), bf16[4,32,768]{2,1,0:T(8,128)(2,1)S(1)}, u32[]{:S(2)}, u32[]{:S(2)}) async-start(bf16[4,32,768]{2,1,0:T(8,128)(2,1)} %all_to_all.194), calls=%async_computation.12 | async-start | bytes 393216 | tf_op jit(solution)/shard_map/all_to_all | solution.py:145
  151.0 1.9 fusion.58
  152.9 3.4 %all-to-all-done.12 = bf16[4,32,768]{2,1,0:T(8,128)(2,1)S(1)} async-done(((bf16[4,32,768]{2,1,0:T(8,128)(2,1)}), bf16[4,32,768]{2,1,0:T(8,128)(2,1)S(1)}, u32[]{:S(2)}, u32[]{:S(2)}) %all-to-all-start.12) | async-done | bytes 196640 | tf_op jit(solution)/shard_map/all_to_all | solution.py:145
  156.3 3.4 %all-to-all-start.13 = ((bf16[4,32,768]{2,1,0:T(8,128)(2,1)}), bf16[4,32,768]{2,1,0:T(8,128)(2,1)S(1)}, u32[]{:S(2)}, u32[]{:S(2)}) async-start(bf16[4,32,768]{2,1,0:T(8,128)(2,1)} %all_to_all.197), calls=%async_computation.13 | async-start | bytes 393216 | tf_op jit(solution)/shard_map/all_to_all | solution.py:148
  159.7 0.7 fusion.10
  160.7 1.0 reshape.116
  161.7 3.3 %all-to-all-done.13 = bf16[4,32,768]{2,1,0:T(8,128)(2,1)S(1)} async-done(((bf16[4,32,768]{2,1,0:T(8,128)(2,1)}), bf16[4,32,768]{2,1,0:T(8,128)(2,1)S(1)}, u32[]{:S(2)}, u32[]{:S(2)}) %all-to-all-start.13) | async-done | bytes 196640 | tf_op jit(solution)/shard_map/all_to_all | solution.py:148
  165.0 3.5 %all-to-all-start.4 = ((bf16[8,16,768]{2,0,1:T(8,128)(2,1)}), bf16[8,16,768]{2,0,1:T(8,128)(2,1)S(1)}, u32[]{:S(2)}, u32[]{:S(2)}) async-start(bf16[8,16,768]{2,0,1:T(8,128)(2,1)} %reshape.116), calls=%async_computation.4 | async-start | bytes 393216 | tf_op jit(solution)/shard_map/all_to_all | solution.py:96
  168.5 0.8 fusion.11
  169.6 1.0 reshape.117
  170.6 5.3 %all-to-all-done.4 = bf16[8,16,768]{2,0,1:T(8,128)(2,1)S(1)} async-done(((bf16[8,16,768]{2,0,1:T(8,128)(2,1)}), bf16[8,16,768]{2,0,1:T(8,128)(2,1)S(1)}, u32[]{:S(2)}, u32[]{:S(2)}) %all-to-all-start.4) | async-done | bytes 196640 | tf_op jit(solution)/shard_map/all_to_all | solution.py:96
  175.9 3.4 %all-to-all-start.5 = ((bf16[8,16,768]{2,0,1:T(8,128)(2,1)}), bf16[8,16,768]{2,0,1:T(8,128)(2,1)S(1)}, u32[]{:S(2)}, u32[]{:S(2)}) async-start(bf16[8,16,768]{2,0,1:T(8,128)(2,1)} %reshape.117), calls=%async_computation.5 | async-start | bytes 393216 | tf_op jit(solution)/shard_map/all_to_all | solution.py:103
  179.3 0.7 fusion.12
  180.3 1.0 reshape.118
  181.3 4.2 %all-to-all-done.5 = bf16[8,16,768]{2,0,1:T(8,128)(2,1)S(1)} async-done(((bf16[8,16,768]{2,0,1:T(8,128)(2,1)}), bf16[8,16,768]{2,0,1:T(8,128)(2,1)S(1)}, u32[]{:S(2)}, u32[]{:S(2)}) %all-to-all-start.5) | async-done | bytes 196640 | tf_op jit(solution)/shard_map/all_to_all | solution.py:103
  185.5 3.4 %all-to-all-start.6 = ((bf16[8,16,768]{2,0,1:T(8,128)(2,1)}), bf16[8,16,768]{2,0,1:T(8,128)(2,1)S(1)}, u32[]{:S(2)}, u32[]{:S(2)}) async-start(bf16[8,16,768]{2,0,1:T(8,128)(2,1)} %reshape.118), calls=%async_computation.6 | async-start | bytes 393216 | tf_op jit(solution)/shard_map/all_to_all | solution.py:110
  188.9 0.8 copy.152
  189.7 0.8 copy.153
  190.5 0.8 copy.154
  191.4 0.8 copy.149
  192.2 0.8 copy.150
  193.1 2.0 %all-to-all-done.6 = bf16[8,16,768]{2,0,1:T(8,128)(2,1)S(1)} async-done(((bf16[8,16,768]{2,0,1:T(8,128)(2,1)}), bf16[8,16,768]{2,0,1:T(8,128)(2,1)S(1)}, u32[]{:S(2)}, u32[]{:S(2)}) %all-to-all-start.6) | async-done | bytes 196640 | tf_op jit(solution)/shard_map/all_to_all | solution.py:110
  195.1 0.8 copy.151
  (22 shorter events, 1.3 us)
Async XLA Ops:
  2.3 4.3 %copy-start = (bf16[32,4,768]{2,1,0:T(4,128)(2,1)S(1)}, bf16[32,4,768]{2,1,0:T(4,128)(2,1)}, u32[]{:S(2)}) copy-start(bf16[32,4,768]{2,1,0:T(4,128)(2,1)} %param.15) | copy-start | bytes 589828
  2.3 9.7 %all-to-all-start.8 = ((bf16[32,4,768]{2,0,1:T(8,128)(2,1)}), bf16[32,4,768]{2,0,1:T(8,128)(2,1)S(1)}, u32[]{:S(2)}, u32[]{:S(2)}) async-start(bf16[32,4,768]{2,0,1:T(8,128)(2,1)} %copy.133), calls=%async_computation.8 | async-start | bytes 393216 | tf_op jit(solution)/shard_map/all_to_all | solution.py:123
  7.3 8.0 %copy-start.1 = (bf16[32,4,768]{2,1,0:T(4,128)(2,1)S(1)}, bf16[32,4,768]{2,1,0:T(4,128)(2,1)}, u32[]{:S(2)}) copy-start(bf16[32,4,768]{2,1,0:T(4,128)(2,1)} %param.14) | copy-start | bytes 589828
  11.9 8.7 %all-to-all-start.9 = ((bf16[32,4,768]{2,0,1:T(8,128)(2,1)}), bf16[32,4,768]{2,0,1:T(8,128)(2,1)S(1)}, u32[]{:S(2)}, u32[]{:S(2)}) async-start(bf16[32,4,768]{2,0,1:T(8,128)(2,1)} %copy.136), calls=%async_computation.9 | async-start | bytes 393216 | tf_op jit(solution)/shard_map/all_to_all | solution.py:129
  16.0 8.0 %copy-start.2 = (bf16[32,4,768]{2,1,0:T(4,128)(2,1)S(1)}, bf16[32,4,768]{2,1,0:T(4,128)(2,1)}, u32[]{:S(2)}) copy-start(bf16[32,4,768]{2,1,0:T(4,128)(2,1)} %param.12) | copy-start | bytes 589828
  20.6 8.7 %all-to-all-start.10 = ((bf16[32,4,768]{2,0,1:T(8,128)(2,1)}), bf16[32,4,768]{2,0,1:T(8,128)(2,1)S(1)}, u32[]{:S(2)}, u32[]{:S(2)}) async-start(bf16[32,4,768]{2,0,1:T(8,128)(2,1)} %copy.137), calls=%async_computation.10 | async-start | bytes 393216 | tf_op jit(solution)/shard_map/all_to_all | solution.py:126
  24.0 13.0 %copy-start.3 = (bf16[32,4,768]{2,1,0:T(4,128)(2,1)S(1)}, bf16[32,4,768]{2,1,0:T(4,128)(2,1)}, u32[]{:S(2)}) copy-start(bf16[32,4,768]{2,1,0:T(4,128)(2,1)} %param.10) | copy-start | bytes 589828
  49.7 9.7 %all-to-all-start.2 = ((bf16[32,4,768]{2,1,0:T(4,128)(2,1)}), bf16[32,4,768]{2,1,0:T(4,128)(2,1)S(1)}, u32[]{:S(2)}, u32[]{:S(2)}) async-start(bf16[32,4,768]{2,1,0:T(4,128)(2,1)} %param.11), calls=%async_computation.2 | async-start | bytes 393216 | tf_op jit(solution)/shard_map/all_to_all | solution.py:64
  59.4 9.6 %all-to-all-start.1 = ((bf16[32,4,768]{2,1,0:T(4,128)(2,1)}), bf16[32,4,768]{2,1,0:T(4,128)(2,1)S(1)}, u32[]{:S(2)}, u32[]{:S(2)}) async-start(bf16[32,4,768]{2,1,0:T(4,128)(2,1)} %param.9), calls=%async_computation.1 | async-start | bytes 393216 | tf_op jit(solution)/shard_map/all_to_all | solution.py:62
  68.9 9.8 %all-to-all-start = ((bf16[32,4,768]{2,1,0:T(4,128)(2,1)}), bf16[32,4,768]{2,1,0:T(4,128)(2,1)S(1)}, u32[]{:S(2)}, u32[]{:S(2)}) async-start(bf16[32,4,768]{2,1,0:T(4,128)(2,1)} %param.8), calls=%async_computation | async-start | bytes 393216 | tf_op jit(solution)/shard_map/all_to_all | solution.py:61
  78.7 68.9 %all-to-all-start.11 = ((bf16[4,32,768]{2,1,0:T(8,128)(2,1)}), bf16[4,32,768]{2,1,0:T(8,128)(2,1)S(1)}, u32[]{:S(2)}, u32[]{:S(2)}) async-start(bf16[4,32,768]{2,1,0:T(8,128)(2,1)} %all_to_all.191), calls=%async_computation.11 | async-start | bytes 393216 | tf_op jit(solution)/shard_map/all_to_all | solution.py:142
  147.6 8.7 %all-to-all-start.12 = ((bf16[4,32,768]{2,1,0:T(8,128)(2,1)}), bf16[4,32,768]{2,1,0:T(8,128)(2,1)S(1)}, u32[]{:S(2)}, u32[]{:S(2)}) async-start(bf16[4,32,768]{2,1,0:T(8,128)(2,1)} %all_to_all.194), calls=%async_computation.12 | async-start | bytes 393216 | tf_op jit(solution)/shard_map/all_to_all | solution.py:145
  156.3 8.7 %all-to-all-start.13 = ((bf16[4,32,768]{2,1,0:T(8,128)(2,1)}), bf16[4,32,768]{2,1,0:T(8,128)(2,1)S(1)}, u32[]{:S(2)}, u32[]{:S(2)}) async-start(bf16[4,32,768]{2,1,0:T(8,128)(2,1)} %all_to_all.197), calls=%async_computation.13 | async-start | bytes 393216 | tf_op jit(solution)/shard_map/all_to_all | solution.py:148
  165.0 10.9 %all-to-all-start.4 = ((bf16[8,16,768]{2,0,1:T(8,128)(2,1)}), bf16[8,16,768]{2,0,1:T(8,128)(2,1)S(1)}, u32[]{:S(2)}, u32[]{:S(2)}) async-start(bf16[8,16,768]{2,0,1:T(8,128)(2,1)} %reshape.116), calls=%async_computation.4 | async-start | bytes 393216 | tf_op jit(solution)/shard_map/all_to_all | solution.py:96
  175.9 9.6 %all-to-all-start.5 = ((bf16[8,16,768]{2,0,1:T(8,128)(2,1)}), bf16[8,16,768]{2,0,1:T(8,128)(2,1)S(1)}, u32[]{:S(2)}, u32[]{:S(2)}) async-start(bf16[8,16,768]{2,0,1:T(8,128)(2,1)} %reshape.117), calls=%async_computation.5 | async-start | bytes 393216 | tf_op jit(solution)/shard_map/all_to_all | solution.py:103
  185.5 9.6 %all-to-all-start.6 = ((bf16[8,16,768]{2,0,1:T(8,128)(2,1)}), bf16[8,16,768]{2,0,1:T(8,128)(2,1)S(1)}, u32[]{:S(2)}, u32[]{:S(2)}) async-start(bf16[8,16,768]{2,0,1:T(8,128)(2,1)} %reshape.118), calls=%async_computation.6 | async-start | bytes 393216 | tf_op jit(solution)/shard_map/all_to_all | solution.py:110
where the time goes:
time: 197 us; the launch traced here: 196 us
  blocking collectives  84.5 us (43%)
  starting transfers between devices  41.6 us (21%)
  waiting for transfers between devices  41.6 us (21%)
  local copies, waits for them, and re-layouts  19.9 us (10%)
  matrix products  5.4 us (3%)
    psum x1, blocking collectives, local(): scores, prob_grad = lax.psum((score_part, prob_part), ('col', 'seq'))  64.1 us
    all_to_all x1, blocking collectives, local(): lax.all_to_all(row_value, 'col', split_axis=0, concat_axis=1, tiled=True)  12.7 us
    unnamed x18, local copies, waits for them, and re-layouts  8.05 us
    all_to_all x1, blocking collectives, local(): lax.all_to_all(col_query.reshape(seq_dev, flat_width), 'seq', split_axis=...  7.69 us
    all_to_all x1, waiting for transfers between devices, local(): lax.all_to_all(row_key, 'col', split_axis=0, concat_axis=1, tiled=True)  5.42 us
    all_to_all x1, waiting for transfers between devices, local(): lax.all_to_all(query_grad.astype(jnp.bfloat16).reshape(own_rows, cols, wi...  5.29 us
    all_to_all x1, waiting for transfers between devices, local(): lax.all_to_all(col_value.reshape(seq_dev, flat_width), 'seq', split_axis=...  5.25 us
    all_to_all x1, waiting for transfers between devices, local(): lax.all_to_all(col_key.reshape(seq_dev, flat_width), 'seq', split_axis=1,...  4.63 us
  transfers between devices with their start and end apart: 12, of which 10 were waited for; matrix products, arithmetic and copies ran while one was open for 11% of the time, Pallas kernels for 0%

commit v1 on v0

--- a/solution.py
+++ b/solution.py
@@ -2,6 +2,7 @@
 import jax.numpy as jnp
 from jax import lax
 from jax.sharding import PartitionSpec as P
+from jax.lax import psum
 
 HEADS = 12
 HEAD = 64
@@ -78,7 +79,7 @@
     prob_part = jnp.einsum(
         "sihe,sjhe->hij", gradient_row_block, value_row_block, preferred_element_type=jnp.float32
     )
-    scores, prob_grad = lax.psum((score_part, prob_part), ("col", "seq"))
+    scores, prob_grad = psum(psum((score_part, prob_part), "seq"), axis_name="col")
     attention_weight_rows, score_gradient_part = tied_terms(scores, prob_grad, row_scale)
     query_grad = jnp.einsum(
         "hij,sjhe->sihe", score_gradient_part, key_row_block, preferred_element_type=jnp.float32

time: 197 us -> 170 us (0.86)
  blocking collectives: 84.5 us -> 56.7 us
    psum x1 -> x2, blocking collectives: 64.1 us -> 36.3 us  [the longest x1 22.4 us: local(): psum(psum((score_part, prob_part), 'seq'), axis_name='col')]
    unnamed x18 -> x22, local copies, waits for them, and re-layouts: 8.05 us -> 8.06 us
  transfers between devices with their start and end apart: 12 -> 12, of which waited for: 10 -> 10; matrix products, arithmetic and copies ran while one was open for 11% -> 13% of each run, Pallas kernels for 0% -> 0%
where the time goes in v1:
time: 170 us; the launch traced here: 168 us
  blocking collectives  56.7 us (33%)
  starting transfers between devices  41.6 us (24%)
  waiting for transfers between devices  41.6 us (24%)
  local copies, waits for them, and re-layouts  19.9 us (12%)
  matrix products  5.4 us (3%)
  other arithmetic  1.93 us (1%)
    psum x1, blocking collectives, local(): psum(psum((score_part, prob_part), 'seq'), axis_name='col')  22.4 us
    psum x1, blocking collectives, local(): psum((score_part, prob_part), 'seq')  13.9 us
    all_to_all x1, blocking collectives, local(): lax.all_to_all(row_query, 'col', split_axis=0, concat_axis=1, tiled=True)  12.7 us
    unnamed x22, local copies, waits for them, and re-layouts  8.06 us
    all_to_all x1, blocking collectives, local(): lax.all_to_all(col_value.reshape(seq_dev, flat_width), 'seq', split_axis=...  7.69 us
    all_to_all x1, waiting for transfers between devices, local(): lax.all_to_all(row_grad, 'col', split_axis=0, concat_axis=1, tiled=True)  5.42 us
    all_to_all x1, waiting for transfers between devices, local(): lax.all_to_all(key_gradient_part.astype(jnp.bfloat16).reshape(own_rows, c...  5.36 us
    all_to_all x1, waiting for transfers between devices, local(): lax.all_to_all(col_grad.reshape(seq_dev, flat_width), 'seq', split_axis=1...  5.25 us
  transfers between devices with their start and end apart: 12, of which 10 were waited for; matrix products, arithmetic and copies ran while one was open for 13% of the time, Pallas kernels for 0%

profile of v1, /device:TPU:0, one launch (start us, length us, event | category | flops | bytes accessed | tf_op | source)
XLA Modules:
  0.0 168.2 jit_solution(10150848662730892218)
XLA Ops:
  0.6 1.6 copy.132
  2.3 4.3 %all-to-all-start.7 = ((bf16[32,4,768]{2,0,1:T(8,128)(2,1)}), bf16[32,4,768]{2,0,1:T(8,128)(2,1)S(1)}, u32[]{:S(2)}, u32[]{:S(2)}) async-start(bf16[32,4,768]{2,0,1:T(8,128)(2,1)} %copy.132), calls=%async_computation.7 | async-start | bytes 393216 | tf_op jit(solution)/shard_map/all_to_all | solution.py:121
  6.6 0.7 copy.133
  7.3 4.6 %all-to-all-done.7 = bf16[32,4,768]{2,0,1:T(8,128)(2,1)S(1)} async-done(((bf16[32,4,768]{2,0,1:T(8,128)(2,1)}), bf16[32,4,768]{2,0,1:T(8,128)(2,1)S(1)}, u32[]{:S(2)}, u32[]{:S(2)}) %all-to-all-start.7) | async-done | bytes 196640 | tf_op jit(solution)/shard_map/all_to_all | solution.py:121
  11.9 3.4 %all-to-all-start.8 = ((bf16[32,4,768]{2,0,1:T(8,128)(2,1)}), bf16[32,4,768]{2,0,1:T(8,128)(2,1)S(1)}, u32[]{:S(2)}, u32[]{:S(2)}) async-start(bf16[32,4,768]{2,0,1:T(8,128)(2,1)} %copy.133), calls=%async_computation.8 | async-start | bytes 393216 | tf_op jit(solution)/shard_map/all_to_all | solution.py:124
  15.3 0.7 copy.136
  16.0 4.6 %all-to-all-done.8 = bf16[32,4,768]{2,0,1:T(8,128)(2,1)S(1)} async-done(((bf16[32,4,768]{2,0,1:T(8,128)(2,1)}), bf16[32,4,768]{2,0,1:T(8,128)(2,1)S(1)}, u32[]{:S(2)}, u32[]{:S(2)}) %all-to-all-start.8) | async-done | bytes 196640 | tf_op jit(solution)/shard_map/all_to_all | solution.py:124
  20.6 3.4 %all-to-all-start.9 = ((bf16[32,4,768]{2,0,1:T(8,128)(2,1)}), bf16[32,4,768]{2,0,1:T(8,128)(2,1)S(1)}, u32[]{:S(2)}, u32[]{:S(2)}) async-start(bf16[32,4,768]{2,0,1:T(8,128)(2,1)} %copy.136), calls=%async_computation.9 | async-start | bytes 393216 | tf_op jit(solution)/shard_map/all_to_all | solution.py:130
  24.0 5.2 %all-to-all-done.9 = bf16[32,4,768]{2,0,1:T(8,128)(2,1)S(1)} async-done(((bf16[32,4,768]{2,0,1:T(8,128)(2,1)}), bf16[32,4,768]{2,0,1:T(8,128)(2,1)S(1)}, u32[]{:S(2)}, u32[]{:S(2)}) %all-to-all-start.9) | async-done | bytes 196640 | tf_op jit(solution)/shard_map/all_to_all | solution.py:130
  29.3 7.7 %all_to_all.214 = bf16[32,4,768]{2,0,1:T(8,128)(2,1)S(1)} all-to-all(bf16[32,4,768]{2,0,1:T(8,128)(2,1)S(1)} %copy.137), channel_id=1, replica_groups=mesh['grp'=2,'col'=4,'seq'=4] {'seq'}, dimensions={1} | all-to-all | bytes 393216 | tf_op jit(solution)/shard_map/all_to_all | solution.py:127
  37.0 12.7 %all_to_all.215 = bf16[32,4,768]{2,1,0:T(4,128)(2,1)S(1)} all-to-all(bf16[32,4,768]{2,1,0:T(4,128)(2,1)S(1)} %copy-done.3), channel_id=1, replica_groups=mesh['grp'=2,'col'=4,'seq'=4] {'col'}, dimensions={0} | all-to-all | bytes 393216 | tf_op jit(solution)/shard_map/all_to_all | solution.py:62
  49.7 3.4 %all-to-all-start.1 = ((bf16[32,4,768]{2,1,0:T(4,128)(2,1)}), bf16[32,4,768]{2,1,0:T(4,128)(2,1)S(1)}, u32[]{:S(2)}, u32[]{:S(2)}) async-start(bf16[32,4,768]{2,1,0:T(4,128)(2,1)} %param.9), calls=%async_computation.1 | async-start | bytes 393216 | tf_op jit(solution)/shard_map/all_to_all | solution.py:63
  53.1 0.3 reshape.107
  53.4 0.4 copy.134
  53.8 0.3 reshape.108
  54.1 0.4 copy.135
  54.5 0.3 reshape.109
  54.8 0.4 copy.138
  55.2 0.3 reshape.110
  55.8 3.5 %all-to-all-done.1 = bf16[32,4,768]{2,1,0:T(4,128)(2,1)S(1)} async-done(((bf16[32,4,768]{2,1,0:T(4,128)(2,1)}), bf16[32,4,768]{2,1,0:T(4,128)(2,1)S(1)}, u32[]{:S(2)}, u32[]{:S(2)}) %all-to-all-start.1) | async-done | bytes 196640 | tf_op jit(solution)/shard_map/all_to_all | solution.py:63
  59.4 3.4 %all-to-all-start.2 = ((bf16[32,4,768]{2,1,0:T(4,128)(2,1)}), bf16[32,4,768]{2,1,0:T(4,128)(2,1)S(1)}, u32[]{:S(2)}, u32[]{:S(2)}) async-start(bf16[32,4,768]{2,1,0:T(4,128)(2,1)} %param.11), calls=%async_computation.2 | async-start | bytes 393216 | tf_op jit(solution)/shard_map/all_to_all | solution.py:65
  62.7 0.4 fusion.59
  63.2 0.3 fusion.15
  63.5 5.4 %all-to-all-done.2 = bf16[32,4,768]{2,1,0:T(4,128)(2,1)S(1)} async-done(((bf16[32,4,768]{2,1,0:T(4,128)(2,1)}), bf16[32,4,768]{2,1,0:T(4,128)(2,1)S(1)}, u32[]{:S(2)}, u32[]{:S(2)}) %all-to-all-start.2) | async-done | bytes 196640 | tf_op jit(solution)/shard_map/all_to_all | solution.py:65
  68.9 3.4 %all-to-all-start.3 = ((bf16[32,4,768]{2,1,0:T(4,128)(2,1)}), bf16[32,4,768]{2,1,0:T(4,128)(2,1)S(1)}, u32[]{:S(2)}, u32[]{:S(2)}) async-start(bf16[32,4,768]{2,1,0:T(4,128)(2,1)} %param.10), calls=%async_computation.3 | async-start | bytes 393216 | tf_op jit(solution)/shard_map/all_to_all | solution.py:64
  72.3 0.4 fusion.13
  72.7 0.4 copy.142
  73.1 1.0 all_to_all.191
  74.1 0.4 copy.145
  74.6 1.0 all_to_all.194
  75.5 0.6 fusion.14
  76.2 0.4 copy.148
  76.6 1.0 all_to_all.197
  77.6 0.3 reshape.100
  78.0 0.3 reshape.101
  78.4 0.3 reshape.102
  78.7 3.4 %all-to-all-start.11 = ((bf16[4,32,768]{2,1,0:T(8,128)(2,1)}), bf16[4,32,768]{2,1,0:T(8,128)(2,1)S(1)}, u32[]{:S(2)}, u32[]{:S(2)}) async-start(bf16[4,32,768]{2,1,0:T(8,128)(2,1)} %all_to_all.191), calls=%async_computation.11 | async-start | bytes 393216 | tf_op jit(solution)/shard_map/all_to_all | solution.py:143
  82.5 0.5 fusion.21
  83.0 0.5 convolution_bitcast_fusion
  83.5 13.9 %all-reduce = (f32[12,16,16]{2,1,0:T(8,128)S(1)}, f32[12,16,16]{2,1,0:T(8,128)S(1)}) all-reduce(f32[12,16,16]{2,1,0:T(8,128)S(1)} %convolution_bitcast_fusion, f32[12,16,16]{2,1,0:T(8,128)S(1)} %fusion.21), channel_id=1, replica_groups=mesh['grp'=2,'col'=4,'seq'=4] {'seq'}, use_global_device_ids=true, to_apply=%region_4.0 | all-reduce | flops 6144 | bytes 49152 | tf_op jit(solution)/shard_map/psum | solution.py:82
  97.4 22.4 %all-reduce.1 = (f32[12,16,16]{2,1,0:T(8,128)S(1)}, f32[12,16,16]{2,1,0:T(8,128)S(1)}) all-reduce(f32[12,16,16]{2,1,0:T(8,128)S(1)} %get-tuple-element.24, f32[12,16,16]{2,1,0:T(8,128)S(1)} %get-tuple-element.25), channel_id=1, replica_groups=mesh['grp'=2,'col'=4,'seq'=4] {'col'}, use_global_device_ids=true, to_apply=%region_5.0 | all-reduce | flops 6144 | bytes 49152 | tf_op jit(solution)/shard_map/psum | solution.py:82
  119.9 3.4 %all-to-all-start.12 = ((bf16[4,32,768]{2,1,0:T(8,128)(2,1)}), bf16[4,32,768]{2,1,0:T(8,128)(2,1)S(1)}, u32[]{:S(2)}, u32[]{:S(2)}) async-start(bf16[4,32,768]{2,1,0:T(8,128)(2,1)} %all_to_all.194), calls=%async_computation.12 | async-start | bytes 393216 | tf_op jit(solution)/shard_map/all_to_all | solution.py:146
  123.3 1.9 %fusion.58 = (f32[12,16]{1,0:T(8,128)S(1)}, f32[12,16,16]{2,1,0:T(8,128)S(1)}) fusion(f32[12,16,16]{2,1,0:T(8,128)S(1)} %get-tuple-element.27), kind=kOutput, calls=%fused_computation.74 | output fusion | flops 6159 | bytes 25344 | tf_op jit(solution)/shard_map/sub | solution.py:12
  125.2 3.4 %all-to-all-done.12 = bf16[4,32,768]{2,1,0:T(8,128)(2,1)S(1)} async-done(((bf16[4,32,768]{2,1,0:T(8,128)(2,1)}), bf16[4,32,768]{2,1,0:T(8,128)(2,1)S(1)}, u32[]{:S(2)}, u32[]{:S(2)}) %all-to-all-start.12) | async-done | bytes 196640 | tf_op jit(solution)/shard_map/all_to_all | solution.py:146
  128.6 3.4 %all-to-all-start.13 = ((bf16[4,32,768]{2,1,0:T(8,128)(2,1)}), bf16[4,32,768]{2,1,0:T(8,128)(2,1)S(1)}, u32[]{:S(2)}, u32[]{:S(2)}) async-start(bf16[4,32,768]{2,1,0:T(8,128)(2,1)} %all_to_all.197), calls=%async_computation.13 | async-start | bytes 393216 | tf_op jit(solution)/shard_map/all_to_all | solution.py:149
  131.9 0.8 fusion.11
  133.1 1.0 reshape.117
  134.0 3.2 %all-to-all-done.13 = bf16[4,32,768]{2,1,0:T(8,128)(2,1)S(1)} async-done(((bf16[4,32,768]{2,1,0:T(8,128)(2,1)}), bf16[4,32,768]{2,1,0:T(8,128)(2,1)S(1)}, u32[]{:S(2)}, u32[]{:S(2)}) %all-to-all-start.13) | async-done | bytes 196640 | tf_op jit(solution)/shard_map/all_to_all | solution.py:149
  137.2 3.5 %all-to-all-start.5 = ((bf16[8,16,768]{2,0,1:T(8,128)(2,1)}), bf16[8,16,768]{2,0,1:T(8,128)(2,1)S(1)}, u32[]{:S(2)}, u32[]{:S(2)}) async-start(bf16[8,16,768]{2,0,1:T(8,128)(2,1)} %reshape.117), calls=%async_computation.5 | async-start | bytes 393216 | tf_op jit(solution)/shard_map/all_to_all | solution.py:104
  140.8 0.7 fusion.10
  141.8 1.0 reshape.116
  142.8 5.4 %all-to-all-done.5 = bf16[8,16,768]{2,0,1:T(8,128)(2,1)S(1)} async-done(((bf16[8,16,768]{2,0,1:T(8,128)(2,1)}), bf16[8,16,768]{2,0,1:T(8,128)(2,1)S(1)}, u32[]{:S(2)}, u32[]{:S(2)}) %all-to-all-start.5) | async-done | bytes 196640 | tf_op jit(solution)/shard_map/all_to_all | solution.py:104
  148.2 3.4 %all-to-all-start.4 = ((bf16[8,16,768]{2,0,1:T(8,128)(2,1)}), bf16[8,16,768]{2,0,1:T(8,128)(2,1)S(1)}, u32[]{:S(2)}, u32[]{:S(2)}) async-start(bf16[8,16,768]{2,0,1:T(8,128)(2,1)} %reshape.116), calls=%async_computation.4 | async-start | bytes 393216 | tf_op jit(solution)/shard_map/all_to_all | solution.py:97
  151.5 0.7 fusion.12
  152.5 1.0 reshape.118
  153.5 4.2 %all-to-all-done.4 = bf16[8,16,768]{2,0,1:T(8,128)(2,1)S(1)} async-done(((bf16[8,16,768]{2,0,1:T(8,128)(2,1)}), bf16[8,16,768]{2,0,1:T(8,128)(2,1)S(1)}, u32[]{:S(2)}, u32[]{:S(2)}) %all-to-all-start.4) | async-done | bytes 196640 | tf_op jit(solution)/shard_map/all_to_all | solution.py:97
  157.8 3.4 %all-to-all-start.6 = ((bf16[8,16,768]{2,0,1:T(8,128)(2,1)}), bf16[8,16,768]{2,0,1:T(8,128)(2,1)S(1)}, u32[]{:S(2)}, u32[]{:S(2)}) async-start(bf16[8,16,768]{2,0,1:T(8,128)(2,1)} %reshape.118), calls=%async_computation.6 | async-start | bytes 393216 | tf_op jit(solution)/shard_map/all_to_all | solution.py:111
  161.1 0.8 copy.152
  162.0 0.8 copy.153
  162.8 0.8 copy.154
  163.6 0.8 copy.150
  164.5 0.8 copy.149
  165.3 2.0 %all-to-all-done.6 = bf16[8,16,768]{2,0,1:T(8,128)(2,1)S(1)} async-done(((bf16[8,16,768]{2,0,1:T(8,128)(2,1)}), bf16[8,16,768]{2,0,1:T(8,128)(2,1)S(1)}, u32[]{:S(2)}, u32[]{:S(2)}) %all-to-all-start.6) | async-done | bytes 196640 | tf_op jit(solution)/shard_map/all_to_all | solution.py:111
  167.4 0.8 copy.151
  (27 shorter events, 1.6 us)
Async XLA Ops:
  2.3 4.3 %copy-start = (bf16[32,4,768]{2,1,0:T(4,128)(2,1)S(1)}, bf16[32,4,768]{2,1,0:T(4,128)(2,1)}, u32[]{:S(2)}) copy-start(bf16[32,4,768]{2,1,0:T(4,128)(2,1)} %param.13) | copy-start | bytes 589828
  2.3 9.7 %all-to-all-start.7 = ((bf16[32,4,768]{2,0,1:T(8,128)(2,1)}), bf16[32,4,768]{2,0,1:T(8,128)(2,1)S(1)}, u32[]{:S(2)}, u32[]{:S(2)}) async-start(bf16[32,4,768]{2,0,1:T(8,128)(2,1)} %copy.132), calls=%async_computation.7 | async-start | bytes 393216 | tf_op jit(solution)/shard_map/all_to_all | solution.py:121
  7.3 8.0 %copy-start.1 = (bf16[32,4,768]{2,1,0:T(4,128)(2,1)S(1)}, bf16[32,4,768]{2,1,0:T(4,128)(2,1)}, u32[]{:S(2)}) copy-start(bf16[32,4,768]{2,1,0:T(4,128)(2,1)} %param.15) | copy-start | bytes 589828
  11.9 8.7 %all-to-all-start.8 = ((bf16[32,4,768]{2,0,1:T(8,128)(2,1)}), bf16[32,4,768]{2,0,1:T(8,128)(2,1)S(1)}, u32[]{:S(2)}, u32[]{:S(2)}) async-start(bf16[32,4,768]{2,0,1:T(8,128)(2,1)} %copy.133), calls=%async_computation.8 | async-start | bytes 393216 | tf_op jit(solution)/shard_map/all_to_all | solution.py:124
  16.0 8.0 %copy-start.2 = (bf16[32,4,768]{2,1,0:T(4,128)(2,1)S(1)}, bf16[32,4,768]{2,1,0:T(4,128)(2,1)}, u32[]{:S(2)}) copy-start(bf16[32,4,768]{2,1,0:T(4,128)(2,1)} %param.14) | copy-start | bytes 589828
  20.6 8.7 %all-to-all-start.9 = ((bf16[32,4,768]{2,0,1:T(8,128)(2,1)}), bf16[32,4,768]{2,0,1:T(8,128)(2,1)S(1)}, u32[]{:S(2)}, u32[]{:S(2)}) async-start(bf16[32,4,768]{2,0,1:T(8,128)(2,1)} %copy.136), calls=%async_computation.9 | async-start | bytes 393216 | tf_op jit(solution)/shard_map/all_to_all | solution.py:130
  24.0 13.0 %copy-start.3 = (bf16[32,4,768]{2,1,0:T(4,128)(2,1)S(1)}, bf16[32,4,768]{2,1,0:T(4,128)(2,1)}, u32[]{:S(2)}) copy-start(bf16[32,4,768]{2,1,0:T(4,128)(2,1)} %param.8) | copy-start | bytes 589828
  49.7 9.7 %all-to-all-start.1 = ((bf16[32,4,768]{2,1,0:T(4,128)(2,1)}), bf16[32,4,768]{2,1,0:T(4,128)(2,1)S(1)}, u32[]{:S(2)}, u32[]{:S(2)}) async-start(bf16[32,4,768]{2,1,0:T(4,128)(2,1)} %param.9), calls=%async_computation.1 | async-start | bytes 393216 | tf_op jit(solution)/shard_map/all_to_all | solution.py:63
  59.4 9.6 %all-to-all-start.2 = ((bf16[32,4,768]{2,1,0:T(4,128)(2,1)}), bf16[32,4,768]{2,1,0:T(4,128)(2,1)S(1)}, u32[]{:S(2)}, u32[]{:S(2)}) async-start(bf16[32,4,768]{2,1,0:T(4,128)(2,1)} %param.11), calls=%async_computation.2 | async-start | bytes 393216 | tf_op jit(solution)/shard_map/all_to_all | solution.py:65
  68.9 9.8 %all-to-all-start.3 = ((bf16[32,4,768]{2,1,0:T(4,128)(2,1)}), bf16[32,4,768]{2,1,0:T(4,128)(2,1)S(1)}, u32[]{:S(2)}, u32[]{:S(2)}) async-start(bf16[32,4,768]{2,1,0:T(4,128)(2,1)} %param.10), calls=%async_computation.3 | async-start | bytes 393216 | tf_op jit(solution)/shard_map/all_to_all | solution.py:64
  78.7 41.1 %all-to-all-start.11 = ((bf16[4,32,768]{2,1,0:T(8,128)(2,1)}), bf16[4,32,768]{2,1,0:T(8,128)(2,1)S(1)}, u32[]{:S(2)}, u32[]{:S(2)}) async-start(bf16[4,32,768]{2,1,0:T(8,128)(2,1)} %all_to_all.191), calls=%async_computation.11 | async-start | bytes 393216 | tf_op jit(solution)/shard_map/all_to_all | solution.py:143
  119.8 12.1 %copy-start.4 = (f32[12,16,16]{2,1,0:T(8,128)}, f32[12,16,16]{2,1,0:T(8,128)S(1)}, u32[]{:S(2)}) copy-start(f32[12,16,16]{2,1,0:T(8,128)S(1)} %get-tuple-element.26) | copy-start | bytes 36868
  119.9 8.7 %all-to-all-start.12 = ((bf16[4,32,768]{2,1,0:T(8,128)(2,1)}), bf16[4,32,768]{2,1,0:T(8,128)(2,1)S(1)}, u32[]{:S(2)}, u32[]{:S(2)}) async-start(bf16[4,32,768]{2,1,0:T(8,128)(2,1)} %all_to_all.194), calls=%async_computation.12 | async-start | bytes 393216 | tf_op jit(solution)/shard_map/all_to_all | solution.py:146
  128.6 8.7 %all-to-all-start.13 = ((bf16[4,32,768]{2,1,0:T(8,128)(2,1)}), bf16[4,32,768]{2,1,0:T(8,128)(2,1)S(1)}, u32[]{:S(2)}, u32[]{:S(2)}) async-start(bf16[4,32,768]{2,1,0:T(8,128)(2,1)} %all_to_all.197), calls=%async_computation.13 | async-start | bytes 393216 | tf_op jit(solution)/shard_map/all_to_all | solution.py:149
  134.0 6.8 %copy-start.5 = (f32[12,16,16]{2,1,0:T(8,128)S(1)}, f32[12,16,16]{2,1,0:T(8,128)}, u32[]{:S(2)}) copy-start(f32[12,16,16]{2,1,0:T(8,128)} %copy-done.4) | copy-start | bytes 36868
  137.2 10.9 %all-to-all-start.5 = ((bf16[8,16,768]{2,0,1:T(8,128)(2,1)}), bf16[8,16,768]{2,0,1:T(8,128)(2,1)S(1)}, u32[]{:S(2)}, u32[]{:S(2)}) async-start(bf16[8,16,768]{2,0,1:T(8,128)(2,1)} %reshape.117), calls=%async_computation.5 | async-start | bytes 393216 | tf_op jit(solution)/shard_map/all_to_all | solution.py:104
  148.2 9.6 %all-to-all-start.4 = ((bf16[8,16,768]{2,0,1:T(8,128)(2,1)}), bf16[8,16,768]{2,0,1:T(8,128)(2,1)S(1)}, u32[]{:S(2)}, u32[]{:S(2)}) async-start(bf16[8,16,768]{2,0,1:T(8,128)(2,1)} %reshape.116), calls=%async_computation.4 | async-start | bytes 393216 | tf_op jit(solution)/shard_map/all_to_all | solution.py:97
  157.8 9.6 %all-to-all-start.6 = ((bf16[8,16,768]{2,0,1:T(8,128)(2,1)}), bf16[8,16,768]{2,0,1:T(8,128)(2,1)S(1)}, u32[]{:S(2)}, u32[]{:S(2)}) async-start(bf16[8,16,768]{2,0,1:T(8,128)(2,1)} %reshape.118), calls=%async_computation.6 | async-start | bytes 393216 | tf_op jit(solution)/shard_map/all_to_all | solution.py:111
